TPU v7x, 128 devices: a whole 4x4x4 slice. The times are simulated.
128 devices in a mesh: ctx: 32 (over y, z, core), exp: 4 (over x).
Axes of the slice: x: 4, y: 4, z: 4, core: 2. Of those that a mesh axis runs over, the one named last changes fastest.
Arguments:
- stream_in: bfloat16 [4096, 6144], P('ctx'), may hold values from -41 to 41
- queries: bfloat16 [4096, 8192], P('ctx', 'exp'), may hold values from -6 to 6
- key_proj: bfloat16 [4096, 8192], P('ctx', 'exp'), may hold values from -0.5390625 to 0.5390625
- values: bfloat16 [4096, 8192], P('ctx', 'exp'), may hold values from -6 to 6
- attn_gate: bfloat16 [4096, 8192], P('ctx', 'exp'), may hold values from -6 to 6
- decay_rates: float32 [64], P('exp'), may hold values from 1.2207031e-05 to 0.05
- attn_gain: float32 [8192], P('exp'), may hold values from 0.25 to 1.75
- out_weight: bfloat16 [8192, 6144], P('exp', 'ctx'), may hold values from -0.0625 to 0.0625
- ffn_gain: float32 [6144], replicated, may hold values from 0.25 to 1.75
- routing: int32 [4096, 2], P('ctx'), may hold values from 0 to 31, as said below
- route_weights: float32 [4096, 2], P('ctx'), may hold values from 0.25 to 1
- w_gate: bfloat16 [4, 6144, 9216], P('exp', None, 'ctx'), may hold values from -0.078125 to 0.078125
- w_up: bfloat16 [4, 6144, 9216], P('exp', None, 'ctx'), may hold values from -0.078125 to 0.078125
- w_down: bfloat16 [4, 9216, 6144], P('exp', 'ctx'), may hold values from -0.0625 to 0.0625
Outputs:
- residual_out: bfloat16 [4096, 6144], P(('ctx', 'exp'))
- expert_out: bfloat16 [32, 4, 8, 6144], P('ctx', 'exp')
Inputs may be any that keep to these rules, and one draw needn't show every extreme that they name: `routing`: the two ids of a row differ and at most one of them is below 4. In each aligned block of 128 rows (one context shard) an id below 4 is named by at most 8 rows; one such id, the same for all blocks, is named by exactly 8 rows in every block.
All inputs are finite; a program needn't handle non-finite values.
Results may differ from a plain program's by a relative error of at most 0.025.
Values may be sent and summed in bfloat16 or wider, within the bound.
A program may use at most 128 MiB of HBM per device.

v0:
```python
import jax
import jax.numpy as jnp
from jax import lax
from jax.sharding import PartitionSpec as P

HIGHEST = lax.Precision.HIGHEST
CTX = ("yz", "core")


def decayed_prefix(local_state, decay_rates, rows_here):
    count = lax.axis_size(CTX)

    def shift(value, step):
        pairs = [(i, i + step) for i in range(count - step)]
        return lax.ppermute(value.astype(jnp.bfloat16), CTX, pairs).astype(jnp.float32)

    running = shift(local_state, 1)
    step = 1
    while step < count:
        factor = jnp.exp(-decay_rates * (rows_here * step))
        running = running + factor[:, None, None] * shift(running, step)
        step *= 2
    return running


def normalize_rows(row_block, ffn_gain):
    wide_rows = row_block.astype(jnp.float32)
    inverse = lax.rsqrt(jnp.mean(wide_rows * wide_rows, axis=1, keepdims=True) + 1e-06)
    return (wide_rows * inverse * ffn_gain[None, :]).astype(jnp.bfloat16)


def per_device(
    stream_in,
    queries,
    key_proj,
    values,
    attn_gate,
    decay_rates,
    attn_gain,
    out_weight,
    ffn_gain,
    routing,
    route_weights,
    w_gate,
    w_up,
    w_down,
):
    rows_here, model_width = stream_in.shape
    head_count = decay_rates.shape[0]
    head_size = queries.shape[1] // head_count
    exp_count = lax.axis_size("exp")
    own_index = lax.axis_index("exp")
    capacity = rows_here // 16
    own_rows = rows_here // exp_count
    per_block = own_rows + capacity
    query_heads = queries.reshape(rows_here, head_count, head_size)
    key_heads = key_proj.reshape(rows_here, head_count, head_size)
    value_heads = values.reshape(rows_here, head_count, head_size)
    positions = jnp.arange(rows_here, dtype=jnp.float32)
    tail_decay = jnp.exp(-decay_rates[None, :] * (rows_here - 1.0 - positions)[:, None])
    weighted_keys = key_heads.astype(jnp.float32) * tail_decay[:, :, None]
    local_state = jnp.einsum(
        "jhd,jhe->hde", weighted_keys, value_heads.astype(jnp.float32), precision=HIGHEST
    )
    prior_state = decayed_prefix(local_state, decay_rates, rows_here)
    scores = jnp.einsum("ihd,jhd->hij", query_heads, key_heads, preferred_element_type=jnp.float32)
    distance = positions[:, None] - positions[None, :]
    decay_mask = jnp.where(
        distance[None] >= 0.0,
        jnp.exp(-decay_rates[:, None, None] * jnp.maximum(distance, 0.0)[None]),
        0.0,
    )
    near_weights = (scores * decay_mask).astype(jnp.bfloat16)
    near_part = jnp.einsum(
        "hij,jhd->ihd", near_weights, value_heads, preferred_element_type=jnp.float32
    )
    lead_decay = jnp.exp(-decay_rates[None, :] * (positions + 1.0)[:, None])
    far_part = jnp.einsum(
        "ihd,hde->ihe",
        query_heads.astype(jnp.float32) * lead_decay[:, :, None],
        prior_state,
        precision=HIGHEST,
    )
    attended = near_part + far_part
    inverse = lax.rsqrt(jnp.mean(attended * attended, axis=2, keepdims=True) + 1e-06)
    normed = (attended * inverse).reshape(rows_here, head_count * head_size)
    mixed_heads = (
        normed * attn_gain[None, :] * jax.nn.sigmoid(attn_gate.astype(jnp.float32))
    ).astype(jnp.bfloat16)
    held_ids = jnp.arange(exp_count, dtype=jnp.int32)
    hit_mask = routing[:, :, None] == held_ids[None, None, :]
    member = jnp.sum(hit_mask.astype(jnp.int32), axis=1)
    gate_of = jnp.sum(jnp.where(hit_mask, route_weights[:, :, None], 0.0), axis=1)
    slot_rank = jnp.cumsum(member, axis=0) - 1
    slot_index = jnp.arange(capacity, dtype=jnp.int32)
    pick_mask = (member[:, :, None] == 1) & (slot_rank[:, :, None] == slot_index[None, None, :])
    selector = pick_mask.reshape(rows_here, exp_count * capacity).T.astype(jnp.bfloat16)
    slot_weight = jnp.sum(jnp.where(pick_mask, gate_of[:, :, None], 0.0), axis=0)
    slot_mixed = jnp.dot(selector, mixed_heads, preferred_element_type=jnp.float32).astype(
        jnp.bfloat16
    )
    row_blocks = jnp.concatenate(
        [mixed_heads.reshape(exp_count, own_rows, -1), slot_mixed.reshape(exp_count, capacity, -1)],
        axis=1,
    )
    stacked = row_blocks.reshape(exp_count * per_block, head_count * head_size)
    pair_rows = lax.all_gather(stacked, "core", axis=0, tiled=True)
    half_weight = lax.all_gather(out_weight, "yz", axis=1, tiled=True)
    half_width = half_weight.shape[1]
    partial_rows = jnp.dot(pair_rows, half_weight, preferred_element_type=jnp.float32)
    partial_term = partial_rows.astype(jnp.bfloat16).reshape(2, exp_count, per_block, half_width)
    swapped = lax.all_to_all(partial_term, "exp", 1, 1, tiled=True)
    head_sum = jnp.sum(swapped.astype(jnp.float32), axis=1)
    by_parity = lax.all_to_all(head_sum, "core", 0, 0, tiled=True)
    block_width = out_weight.shape[1]
    projected = (
        by_parity.reshape(2, per_block, half_width // block_width, block_width)
        .transpose(1, 2, 0, 3)
        .reshape(per_block, model_width)
    )
    stream_own = lax.dynamic_slice_in_dim(stream_in, own_index * own_rows, own_rows, 0)
    own_selector = lax.dynamic_slice_in_dim(selector, own_index * capacity, capacity, 0)
    stream_slots = jnp.dot(own_selector, stream_in, preferred_element_type=jnp.float32)
    residual_rows = jnp.concatenate([stream_own.astype(jnp.float32), stream_slots], axis=0)
    hidden_rows = (residual_rows + projected).astype(jnp.bfloat16)
    residual_out = hidden_rows[:own_rows]
    slot_hidden = hidden_rows[own_rows:]
    outgoing = normalize_rows(slot_hidden, ffn_gain)
    ctx_count = lax.axis_size(CTX)
    row_piece = lax.all_gather(outgoing, CTX, axis=0, tiled=True)
    gate_part = jnp.dot(row_piece, w_gate[0], preferred_element_type=jnp.float32)
    up_part = jnp.dot(row_piece, w_up[0], preferred_element_type=jnp.float32)
    activated = (jax.nn.silu(gate_part) * up_part).astype(jnp.bfloat16)
    down_part = jnp.dot(activated, w_down[0], preferred_element_type=jnp.float32)
    down_blocks = lax.all_to_all(
        down_part.astype(jnp.bfloat16).reshape(ctx_count, capacity, model_width),
        CTX,
        0,
        0,
        tiled=True,
    )
    summed_down = jnp.sum(down_blocks.astype(jnp.float32), axis=0)
    own_weight = lax.dynamic_index_in_dim(slot_weight, own_index, 0, keepdims=False)
    expert_out = (
        (summed_down * own_weight[:, None])
        .astype(jnp.bfloat16)
        .reshape(1, 1, capacity, model_width)
    )
    return (residual_out, expert_out)


def solution(mesh):
    ctx_size, exp_size = mesh.devices.shape
    split = jax.sharding.Mesh(
        mesh.devices.reshape(ctx_size // 2, 2, exp_size), ("yz", "core", "exp")
    )
    return jax.shard_map(
        per_device,
        mesh=split,
        in_specs=(
            P(CTX, None),
            P(CTX, "exp"),
            P(CTX, "exp"),
            P(CTX, "exp"),
            P(CTX, "exp"),
            P("exp"),
            P("exp"),
            P("exp", CTX),
            P(),
            P(CTX, None),
            P(CTX, None),
            P("exp", None, CTX),
            P("exp", None, CTX),
            P("exp", CTX, None),
        ),
        out_specs=(P((CTX[0], CTX[1], "exp"), None), P(CTX, "exp", None, None)),
        check_vma=False,
    )
```

profile of v0, /device:TPU:1, one launch (start us, length us, event | category | flops | bytes accessed | tf_op | source)
XLA Modules:
  0.0 395.3 jit_solution(3186503120921249758)
XLA Ops:
  9.3 2.1 copy.74
  14.0 4.9 %collective-permute-start = (bf16[16,128,128]{2,1,0:T(8,128)(2,1)S(1)}, bf16[16,128,128]{2,1,0:T(8,128)(2,1)S(1)}, u32[]{:S(2)}, u32[]{:S(2)}) collective-permute-start(bf16[16,128,128]{2,1,0:T(8,128)(2,1)S(1)} %convolution_convert_fusion.3), channel_id=1, source_target_pairs={{0,4},{4,8},{8,12},{12,16},{16,20},{20,24},{24,28},{28,32},{32,36}... | collective-permute-start | bytes 1572872 | tf_op jit(solution)/shard_map/ppermute | solution.py:15
  18.9 6.1 %collective-permute-done = bf16[16,128,128]{2,1,0:T(8,128)(2,1)S(1)} collective-permute-done((bf16[16,128,128]{2,1,0:T(8,128)(2,1)S(1)}, bf16[16,128,128]{2,1,0:T(8,128)(2,1)S(1)}, u32[]{:S(2)}, u32[]{:S(2)}) %collective-permute-start) | collective-permute-done | bytes 524320 | tf_op jit(solution)/shard_map/ppermute | solution.py:15
  25.0 4.4 %collective-permute-start.1 = (bf16[16,128,128]{2,1,0:T(8,128)(2,1)S(1)}, bf16[16,128,128]{2,1,0:T(8,128)(2,1)S(1)}, u32[]{:S(2)}, u32[]{:S(2)}) collective-permute-start(bf16[16,128,128]{2,1,0:T(8,128)(2,1)S(1)} %collective-permute-done), channel_id=1, source_target_pairs={{0,4},{4,8},{8,12},{12,16},{16,20},{20,24},{24,28},{28,32},{32,36}... | collective-permute-start | bytes 1572872 | tf_op jit(solution)/shard_map/ppermute | solution.py:15
  29.4 6.1 %collective-permute-done.1 = bf16[16,128,128]{2,1,0:T(8,128)(2,1)S(1)} collective-permute-done((bf16[16,128,128]{2,1,0:T(8,128)(2,1)S(1)}, bf16[16,128,128]{2,1,0:T(8,128)(2,1)S(1)}, u32[]{:S(2)}, u32[]{:S(2)}) %collective-permute-start.1) | collective-permute-done | bytes 524320 | tf_op jit(solution)/shard_map/ppermute | solution.py:15
  35.8 3.6 collective-permute-start.2
  39.4 10.2 %collective-permute-done.2 = bf16[16,128,128]{2,1,0:T(8,128)(2,1)S(1)} collective-permute-done((bf16[16,128,128]{2,1,0:T(8,128)(2,1)S(1)}, bf16[16,128,128]{2,1,0:T(8,128)(2,1)S(1)}, u32[]{:S(2)}, u32[]{:S(2)}) %collective-permute-start.2) | collective-permute-done | bytes 524320 | tf_op jit(solution)/shard_map/ppermute | solution.py:15
  50.0 6.1 %collective-permute-start.3 = (bf16[16,128,128]{2,1,0:T(8,128)(2,1)S(1)}, bf16[16,128,128]{2,1,0:T(8,128)(2,1)S(1)}, u32[]{:S(2)}, u32[]{:S(2)}) collective-permute-start(bf16[16,128,128]{2,1,0:T(8,128)(2,1)S(1)} %fusion.69), channel_id=1, source_target_pairs={{0,16},{4,20},{8,24},{12,28},{16,32},{20,36},{24,40},{28,44},{32,4... | collective-permute-start | bytes 1572872 | tf_op jit(solution)/shard_map/ppermute | solution.py:15
  56.1 9.6 %collective-permute-done.3 = bf16[16,128,128]{2,1,0:T(8,128)(2,1)S(1)} collective-permute-done((bf16[16,128,128]{2,1,0:T(8,128)(2,1)S(1)}, bf16[16,128,128]{2,1,0:T(8,128)(2,1)S(1)}, u32[]{:S(2)}, u32[]{:S(2)}) %collective-permute-start.3) | collective-permute-done | bytes 524320 | tf_op jit(solution)/shard_map/ppermute | solution.py:15
  67.0 4.0 %collective-permute-start.4 = (bf16[16,128,128]{2,1,0:T(8,128)(2,1)}, bf16[16,128,128]{2,1,0:T(8,128)(2,1)}, u32[]{:S(2)}, u32[]{:S(2)}) collective-permute-start(bf16[16,128,128]{2,1,0:T(8,128)(2,1)} %fusion.27), channel_id=1, source_target_pairs={{0,32},{4,36},{8,40},{12,44},{16,48},{20,52},{24,56},{28,60},{32,6... | collective-permute-start | bytes 1572872 | tf_op jit(solution)/shard_map/ppermute | solution.py:15
  75.5 3.1 collective-permute-done.4
  78.6 3.1 fusion.68
  81.7 4.1 %collective-permute-start.5 = (bf16[16,128,128]{2,1,0:T(8,128)(2,1)}, bf16[16,128,128]{2,1,0:T(8,128)(2,1)}, u32[]{:S(2)}, u32[]{:S(2)}) collective-permute-start(bf16[16,128,128]{2,1,0:T(8,128)(2,1)} %fusion.68), channel_id=1, source_target_pairs={{0,64},{4,68},{8,72},{12,76},{16,80},{20,84},{24,88},{28,92},{32,9... | collective-permute-start | bytes 1572872 | tf_op jit(solution)/shard_map/ppermute | solution.py:15
  89.8 3.1 convolution_bitcast_fusion.1
  92.9 5.1 %multiply_reduce_fusion = (f32[128,16]{0,1:T(8,128)S(1)}, f32[128,16,128]{0,2,1:T(8,128)S(1)}) fusion(f32[128,16,128]{0,2,1:T(8,128)} %convolution_bitcast_fusion.1, f32[128,16]{0,1:T(8,128)S(1)} %get-tuple-element.8, bf16[16,128,128]{2,1,0:T(8,128)(2,1)} %collective-permute-done.5, f32[16]{0:T(128)} %get-tuple-element.2, ...), kind=kOutput, calls=%fused_computation.21 | convolution fusion | flops 408156160 | bytes 5783872 | tf_op jit(solution)/shard_map/ihd,hde->ihe/dot_general | solution.py:78
  99.1 2.6 copy.70
  105.9 22.1 %all-gather.4.cloned.1.call-done = bf16[320,2048]{1,0:T(8,128)(2,1)} async-done(((bf16[160,2048]{1,0:T(8,128)(2,1)}), bf16[320,2048]{1,0:T(8,128)(2,1)}) %all-gather.4.cloned.1.call-update) | async-done | bytes 1310736 | tf_op jit(solution)/shard_map/all_gather | solution.py:107
  128.0 93.3 %all-gather.6.cloned.1.call-done = bf16[2048,3072]{0,1:T(8,128)(2,1)} async-done(((bf16[2048,192]{0,1:T(8,128)(2,1)}), bf16[2048,3072]{0,1:T(8,128)(2,1)}) %all-gather.6.cloned.1.call-update) | async-done | bytes 12582928 | tf_op jit(solution)/shard_map/all_gather | solution.py:108
  221.2 9.2 %convolution_convert_fusion.1 = bf16[320,3072]{1,0:T(8,128)(2,1)S(1)} fusion(bf16[320,2048]{1,0:T(8,128)(2,1)} %all-gather.4.cloned.1.call-done, bf16[2048,3072]{0,1:T(8,128)(2,1)} %all-gather.6.cloned.1.call-done), kind=kOutput, calls=%fused_computation.3 | convolution fusion | flops 4027514880 | bytes 15859712 | tf_op jit(solution)/shard_map/dot_general | solution.py:110
  231.9 4.4 %all-to-all-start = ((bf16[2,4,40,3072]{3,2,0,1:T(8,128)(2,1)}), bf16[2,4,40,3072]{3,2,0,1:T(8,128)(2,1)}, u32[]{:S(2)}, u32[]{:S(2)}) async-start(bf16[2,4,40,3072]{3,2,0,1:T(8,128)(2,1)} %copy.71), calls=%async_computation | async-start | bytes 3932160 | tf_op jit(solution)/shard_map/all_to_all | solution.py:112
  236.5 2.4 fusion.61
  240.8 19.9 %all-to-all-done = bf16[2,4,40,3072]{3,2,0,1:T(8,128)(2,1)} async-done(((bf16[2,4,40,3072]{3,2,0,1:T(8,128)(2,1)}), bf16[2,4,40,3072]{3,2,0,1:T(8,128)(2,1)}, u32[]{:S(2)}, u32[]{:S(2)}) %all-to-all-start) | async-done | bytes 1966112 | tf_op jit(solution)/shard_map/all_to_all | solution.py:112
  262.7 6.6 %all_to_all.15 = f32[2,40,3072]{2,1,0:T(8,128)} all-to-all(f32[2,40,3072]{2,1,0:T(8,128)S(1)} %convert_reduce_fusion.1), channel_id=1, replica_groups=mesh['yz'=16,'core'=2,'exp'=4] {'core'}, dimensions={0} | all-to-all | bytes 1966080 | tf_op jit(solution)/shard_map/all_to_all | solution.py:114
  269.3 2.9 reshape.210
  272.2 3.5 copy.72
  275.7 3.6 reshape.211
  283.2 43.2 %all-gather.8.cloned.1.call-done = bf16[256,6144]{1,0:T(8,128)(2,1)} async-done(((bf16[8,6144]{1,0:T(8,128)(2,1)}), bf16[256,6144]{1,0:T(8,128)(2,1)}) %all-gather.8.cloned.1.call-update) | async-done | bytes 3145744 | tf_op jit(solution)/shard_map/all_gather | solution.py:130
  326.3 4.8 %fusion.4 = f32[256,288]{0,1:T(8,128)} fusion(bf16[256,6144]{1,0:T(8,128)(2,1)} %all-gather.8.cloned.1.call-done, bf16[1,6144,288]{1,2,0:T(8,128)(2,1)} %param.25), kind=kOutput, calls=%fused_computation.8 | convolution fusion | flops 905969664 | bytes 6979584 | tf_op jit(solution)/shard_map/dot_general | solution.py:131
  331.1 9.4 %fusion = bf16[32,8,6144]{2,1,0:T(8,128)(2,1)} fusion(bf16[1,288,6144]{2,1,0:T(8,128)(2,1)S(1)} %copy-done, bf16[256,6144]{1,0:T(8,128)(2,1)} %all-gather.8.cloned.1.call-done, bf16[1,6144,288]{1,2,0:T(8,128)(2,1)} %param.26, f32[256,288]{0,1:T(8,128)} %fusion.4), kind=kOutput, calls=%fused_computation.1 | convolution fusion | flops 1813954560 | bytes 13664256 | tf_op jit(solution)/shard_map/dot_general | solution.py:134
  340.5 5.4 %all-to-all-start.2 = ((bf16[32,8,6144]{2,1,0:T(8,128)(2,1)}), bf16[32,8,6144]{2,1,0:T(8,128)(2,1)}, u32[]{:S(2)}, u32[]{:S(2)}) async-start(bf16[32,8,6144]{2,1,0:T(8,128)(2,1)} %fusion), calls=%async_computation.2 | async-start | bytes 6291456 | tf_op jit(solution)/shard_map/all_to_all | solution.py:135
  347.8 37.9 %all-to-all-done.2 = bf16[32,8,6144]{2,1,0:T(8,128)(2,1)} async-done(((bf16[32,8,6144]{2,1,0:T(8,128)(2,1)}), bf16[32,8,6144]{2,1,0:T(8,128)(2,1)}, u32[]{:S(2)}, u32[]{:S(2)}) %all-to-all-start.2) | async-done | bytes 3145760 | tf_op jit(solution)/shard_map/all_to_all | solution.py:135
  385.8 2.3 convert_reduce_fusion
  (72 shorter events, 32.4 us)
Async XLA Ops:
  7.2 324.0 %copy-start = (bf16[1,288,6144]{2,1,0:T(8,128)(2,1)S(1)}, bf16[1,288,6144]{2,1,0:T(8,128)(2,1)}, u32[]{:S(2)}) copy-start(bf16[1,288,6144]{2,1,0:T(8,128)(2,1)} %param.27) | copy-start | bytes 10616836
  7.2 120.8 %all-gather.4.cloned.1.call-start = ((), (), s32[]{:S(2)}) async-start(), calls=%async_computation.3 | async-start | bytes 1966080 | tf_op jit(solution)/shard_map/all_gather | solution.py:107
  9.3 56.5 %copy-start.7 = (f32[16]{0:T(128)}, f32[16]{0:T(128)S(1)}, u32[]{:S(2)}) copy-start(f32[16]{0:T(128)S(1)} %get-tuple-element.4) | copy-start | bytes 196
  9.3 69.3 %copy-start.6 = (f32[16]{0:T(128)}, f32[16]{0:T(128)S(1)}, u32[]{:S(2)}) copy-start(f32[16]{0:T(128)S(1)} %get-tuple-element.3) | copy-start | bytes 196
  11.3 54.4 %copy-start.10 = (f32[16]{0:T(128)S(1)}, f32[16]{0:T(128)}, u32[]{:S(2)}) copy-start(f32[16]{0:T(128)} %get-tuple-element.5) | copy-start | bytes 196
  14.0 11.0 %collective-permute-start = (bf16[16,128,128]{2,1,0:T(8,128)(2,1)S(1)}, bf16[16,128,128]{2,1,0:T(8,128)(2,1)S(1)}, u32[]{:S(2)}, u32[]{:S(2)}) collective-permute-start(bf16[16,128,128]{2,1,0:T(8,128)(2,1)S(1)} %convolution_convert_fusion.3), channel_id=1, source_target_pairs={{0,4},{4,8},{8,12},{12,16},{16,20},{20,24},{24,28},{28,32},{32,36}... | collective-permute-start | bytes 1572872 | tf_op jit(solution)/shard_map/ppermute | solution.py:15
  25.0 42.0 %copy-start.1 = (bf16[16,128,128]{2,1,0:T(8,128)(2,1)}, bf16[16,128,128]{2,1,0:T(8,128)(2,1)S(1)}, u32[]{:S(2)}) copy-start(bf16[16,128,128]{2,1,0:T(8,128)(2,1)S(1)} %collective-permute-done) | copy-start | bytes 1572868
  25.0 10.5 %collective-permute-start.1 = (bf16[16,128,128]{2,1,0:T(8,128)(2,1)S(1)}, bf16[16,128,128]{2,1,0:T(8,128)(2,1)S(1)}, u32[]{:S(2)}, u32[]{:S(2)}) collective-permute-start(bf16[16,128,128]{2,1,0:T(8,128)(2,1)S(1)} %collective-permute-done), channel_id=1, source_target_pairs={{0,4},{4,8},{8,12},{12,16},{16,20},{20,24},{24,28},{28,32},{32,36}... | collective-permute-start | bytes 1572872 | tf_op jit(solution)/shard_map/ppermute | solution.py:15
  35.5 31.5 %copy-start.2 = (bf16[16,128,128]{2,1,0:T(8,128)(2,1)}, bf16[16,128,128]{2,1,0:T(8,128)(2,1)S(1)}, u32[]{:S(2)}) copy-start(bf16[16,128,128]{2,1,0:T(8,128)(2,1)S(1)} %collective-permute-done.1) | copy-start | bytes 1572868
  35.5 35.5 %copy-start.12 = (s32[128,2]{0,1:T(2,128)S(1)}, s32[128,2]{0,1:T(2,128)}, u32[]{:S(2)}) copy-start(s32[128,2]{0,1:T(2,128)} %param.23) | copy-start | bytes 3076
  35.8 13.8 %collective-permute-start.2 = (bf16[16,128,128]{2,1,0:T(8,128)(2,1)S(1)}, bf16[16,128,128]{2,1,0:T(8,128)(2,1)S(1)}, u32[]{:S(2)}, u32[]{:S(2)}) collective-permute-start(bf16[16,128,128]{2,1,0:T(8,128)(2,1)S(1)} %fusion.26), channel_id=1, source_target_pairs={{0,8},{4,12},{8,16},{12,20},{16,24},{20,28},{24,32},{28,36},{32,40... | collective-permute-start | bytes 1572872 | tf_op jit(solution)/shard_map/ppermute | solution.py:15
  49.6 21.5 %copy-start.3 = (bf16[16,128,128]{2,1,0:T(8,128)(2,1)}, bf16[16,128,128]{2,1,0:T(8,128)(2,1)S(1)}, u32[]{:S(2)}) copy-start(bf16[16,128,128]{2,1,0:T(8,128)(2,1)S(1)} %collective-permute-done.2) | copy-start | bytes 1572868
  50.0 15.7 %collective-permute-start.3 = (bf16[16,128,128]{2,1,0:T(8,128)(2,1)S(1)}, bf16[16,128,128]{2,1,0:T(8,128)(2,1)S(1)}, u32[]{:S(2)}, u32[]{:S(2)}) collective-permute-start(bf16[16,128,128]{2,1,0:T(8,128)(2,1)S(1)} %fusion.69), channel_id=1, source_target_pairs={{0,16},{4,20},{8,24},{12,28},{16,32},{20,36},{24,40},{28,44},{32,4... | collective-permute-start | bytes 1572872 | tf_op jit(solution)/shard_map/ppermute | solution.py:15
  65.7 5.3 %copy-start.4 = (bf16[16,128,128]{2,1,0:T(8,128)(2,1)}, bf16[16,128,128]{2,1,0:T(8,128)(2,1)S(1)}, u32[]{:S(2)}) copy-start(bf16[16,128,128]{2,1,0:T(8,128)(2,1)S(1)} %collective-permute-done.3) | copy-start | bytes 1572868
  67.0 11.6 %collective-permute-start.4 = (bf16[16,128,128]{2,1,0:T(8,128)(2,1)}, bf16[16,128,128]{2,1,0:T(8,128)(2,1)}, u32[]{:S(2)}, u32[]{:S(2)}) collective-permute-start(bf16[16,128,128]{2,1,0:T(8,128)(2,1)} %fusion.27), channel_id=1, source_target_pairs={{0,32},{4,36},{8,40},{12,44},{16,48},{20,52},{24,56},{28,60},{32,6... | collective-permute-start | bytes 1572872 | tf_op jit(solution)/shard_map/ppermute | solution.py:15
  81.7 11.2 %collective-permute-start.5 = (bf16[16,128,128]{2,1,0:T(8,128)(2,1)}, bf16[16,128,128]{2,1,0:T(8,128)(2,1)}, u32[]{:S(2)}, u32[]{:S(2)}) collective-permute-start(bf16[16,128,128]{2,1,0:T(8,128)(2,1)} %fusion.68), channel_id=1, source_target_pairs={{0,64},{4,68},{8,72},{12,76},{16,80},{20,84},{24,88},{28,92},{32,9... | collective-permute-start | bytes 1572872 | tf_op jit(solution)/shard_map/ppermute | solution.py:15
  97.9 3.7 copy-start.8
  98.0 5.3 %copy-start.9 = (pred[128,4]{0,1:T(4,128)(4,1)S(1)}, pred[128,4]{0,1:T(4,128)(4,1)}, u32[]{:S(2)}) copy-start(pred[128,4]{0,1:T(4,128)(4,1)} %broadcast_compare_fusion) | copy-start | bytes 1540
  105.1 116.1 %all-gather.6.cloned.1.call-start = ((), (), s32[]{:S(2)}) async-start(), calls=%async_computation.4 | async-start | bytes 13369344 | tf_op jit(solution)/shard_map/all_gather | solution.py:108
  230.5 5.9 %copy-start.11 = (s32[32]{0:T(128)S(1)}, s32[32]{0:T(128)}, u32[]{:S(2)}) copy-start(s32[32]{0:T(128)} %eq.56) | copy-start | bytes 388
  231.9 28.8 %all-to-all-start = ((bf16[2,4,40,3072]{3,2,0,1:T(8,128)(2,1)}), bf16[2,4,40,3072]{3,2,0,1:T(8,128)(2,1)}, u32[]{:S(2)}, u32[]{:S(2)}) async-start(bf16[2,4,40,3072]{3,2,0,1:T(8,128)(2,1)} %copy.71), calls=%async_computation | async-start | bytes 3932160 | tf_op jit(solution)/shard_map/all_to_all | solution.py:112
  236.3 90.0 %all-gather.8.cloned.1.call-start = ((), (), s32[]{:S(2)}) async-start(), calls=%async_computation.5 | async-start | bytes 3244032 | tf_op jit(solution)/shard_map/all_gather | solution.py:130
  280.9 0.8 copy-start.5
  340.5 5.5 %copy-start.13 = (s32[128,2]{0,1:T(2,128)S(1)}, s32[128,2]{0,1:T(2,128)}, u32[]{:S(2)}) copy-start(s32[128,2]{0,1:T(2,128)} %param.23) | copy-start | bytes 3076
  340.5 5.5 %copy-start.14 = (f32[128,2]{0,1:T(2,128)S(1)}, f32[128,2]{0,1:T(2,128)}, u32[]{:S(2)}) copy-start(f32[128,2]{0,1:T(2,128)} %param.24) | copy-start | bytes 3076
  340.5 45.3 %all-to-all-start.2 = ((bf16[32,8,6144]{2,1,0:T(8,128)(2,1)}), bf16[32,8,6144]{2,1,0:T(8,128)(2,1)}, u32[]{:S(2)}, u32[]{:S(2)}) async-start(bf16[32,8,6144]{2,1,0:T(8,128)(2,1)} %fusion), calls=%async_computation.2 | async-start | bytes 6291456 | tf_op jit(solution)/shard_map/all_to_all | solution.py:135
Sparse Core Ops, SparseCore 0:
  105.2 22.6 all-gather.3
  130.1 91.0 all-gather.5
  283.3 42.9 all-gather.7
where the time goes:
time: 397 us; the launch traced here: 395 us
  waiting for transfers between devices  252 us (63%)
  starting transfers between devices  37.3 us (9%)
  matrix products  36.7 us (9%)
  other arithmetic  26.8 us (7%)
  local copies, waits for them, and re-layouts  22 us (6%)
  between operations  14 us (4%)
  blocking collectives  6.59 us (2%)
    all_gather x1, waiting for transfers between devices, per_device(): half_weight = lax.all_gather(out_weight, 'yz', axis=1, tiled=True)  93.3 us
    all_gather x1, waiting for transfers between devices, per_device(): row_piece = lax.all_gather(outgoing, CTX, axis=0, tiled=True)  43.2 us
    all_to_all x1, waiting for transfers between devices, per_device(): lax.all_to_all(down_part.astype(jnp.bfloat16).reshape(ctx_count, capacity...  37.9 us
    ppermute x6, waiting for transfers between devices, shift(): lax.ppermute(value.astype(jnp.bfloat16), CTX, pairs).astype(jnp.float32)  35.1 us
    ppermute x6, starting transfers between devices, shift(): lax.ppermute(value.astype(jnp.bfloat16), CTX, pairs).astype(jnp.float32)  27.1 us
    all_gather x1, waiting for transfers between devices, per_device(): pair_rows = lax.all_gather(stacked, 'core', axis=0, tiled=True)  22.1 us
    all_to_all x1, waiting for transfers between devices, per_device(): swapped = lax.all_to_all(partial_term, 'exp', 1, 1, tiled=True)  19.9 us
    dot_general x1, matrix products, per_device(): jnp.dot(activated, w_down[0], preferred_element_type=jnp.float32)  9.36 us
  transfers between devices with their start and end apart: 11, of which 10 were waited for; matrix products, arithmetic and copies ran while one was open for 5% of the time, Pallas kernels for 0%

commit v1 on v0

--- a/solution.py
+++ b/solution.py
@@ -109,7 +109,9 @@
     half_width = half_weight.shape[1]
     partial_rows = jnp.dot(pair_rows, half_weight, preferred_element_type=jnp.float32)
     partial_term = partial_rows.astype(jnp.bfloat16).reshape(2, exp_count, per_block, half_width)
-    swapped = lax.all_to_all(partial_term, "exp", 1, 1, tiled=True)
+    shards = jnp.split(partial_term, lax.axis_size("exp"), axis=1)
+    received = lax.all_to_all(jnp.stack(shards), "exp", 0, 0)
+    swapped = jnp.concatenate(received, axis=1)
     head_sum = jnp.sum(swapped.astype(jnp.float32), axis=1)
     by_parity = lax.all_to_all(head_sum, "core", 0, 0, tiled=True)
     block_width = out_weight.shape[1]

time: 397 us -> 397 us (level)
  transfers between devices with their start and end apart: 11 -> 11, of which waited for: 10 -> 10; matrix products, arithmetic and copies ran while one was open for 5% -> 4% of each run, Pallas kernels for 0% -> 0%
where the time goes in v1:
time: 397 us; the launch traced here: 396 us
  waiting for transfers between devices  252 us (63%)
  starting transfers between devices  37.2 us (9%)
  matrix products  36.7 us (9%)
  other arithmetic  28.3 us (7%)
  local copies, waits for them, and re-layouts  20.7 us (5%)
  between operations  14 us (4%)
  blocking collectives  6.6 us (2%)
    all_gather x1, waiting for transfers between devices, per_device(): half_weight = lax.all_gather(out_weight, 'yz', axis=1, tiled=True)  93.3 us
    all_gather x1, waiting for transfers between devices, per_device(): row_piece = lax.all_gather(outgoing, CTX, axis=0, tiled=True)  43.2 us
    all_to_all x1, waiting for transfers between devices, per_device(): lax.all_to_all(down_part.astype(jnp.bfloat16).reshape(ctx_count, capacity...  37.9 us
    ppermute x6, waiting for transfers between devices, shift(): lax.ppermute(value.astype(jnp.bfloat16), CTX, pairs).astype(jnp.float32)  35.1 us
    ppermute x6, starting transfers between devices, shift(): lax.ppermute(value.astype(jnp.bfloat16), CTX, pairs).astype(jnp.float32)  27.1 us
    all_gather x1, waiting for transfers between devices, per_device(): pair_rows = lax.all_gather(stacked, 'core', axis=0, tiled=True)  22.1 us
    all_to_all x1, waiting for transfers between devices, per_device(): received = lax.all_to_all(jnp.stack(shards), 'exp', 0, 0)  19.9 us
    dot_general x1, matrix products, per_device(): jnp.dot(activated, w_down[0], preferred_element_type=jnp.float32)  9.37 us
  transfers between devices with their start and end apart: 11, of which 10 were waited for; matrix products, arithmetic and copies ran while one was open for 4% of the time, Pallas kernels for 0%

profile of v1, /device:TPU:1, one launch (start us, length us, event | category | flops | bytes accessed | tf_op | source)
XLA Modules:
  0.0 395.6 jit_solution(17062926749366474211)
XLA Ops:
  9.3 2.0 copy.74
  14.0 4.9 %collective-permute-start = (bf16[16,128,128]{2,1,0:T(8,128)(2,1)S(1)}, bf16[16,128,128]{2,1,0:T(8,128)(2,1)S(1)}, u32[]{:S(2)}, u32[]{:S(2)}) collective-permute-start(bf16[16,128,128]{2,1,0:T(8,128)(2,1)S(1)} %convolution_convert_fusion.3), channel_id=1, source_target_pairs={{0,4},{4,8},{8,12},{12,16},{16,20},{20,24},{24,28},{28,32},{32,36}... | collective-permute-start | bytes 1572872 | tf_op jit(solution)/shard_map/ppermute | solution.py:15
  18.9 6.1 %collective-permute-done = bf16[16,128,128]{2,1,0:T(8,128)(2,1)S(1)} collective-permute-done((bf16[16,128,128]{2,1,0:T(8,128)(2,1)S(1)}, bf16[16,128,128]{2,1,0:T(8,128)(2,1)S(1)}, u32[]{:S(2)}, u32[]{:S(2)}) %collective-permute-start) | collective-permute-done | bytes 524320 | tf_op jit(solution)/shard_map/ppermute | solution.py:15
  25.0 4.4 %collective-permute-start.1 = (bf16[16,128,128]{2,1,0:T(8,128)(2,1)S(1)}, bf16[16,128,128]{2,1,0:T(8,128)(2,1)S(1)}, u32[]{:S(2)}, u32[]{:S(2)}) collective-permute-start(bf16[16,128,128]{2,1,0:T(8,128)(2,1)S(1)} %collective-permute-done), channel_id=1, source_target_pairs={{0,4},{4,8},{8,12},{12,16},{16,20},{20,24},{24,28},{28,32},{32,36}... | collective-permute-start | bytes 1572872 | tf_op jit(solution)/shard_map/ppermute | solution.py:15
  29.4 6.1 %collective-permute-done.1 = bf16[16,128,128]{2,1,0:T(8,128)(2,1)S(1)} collective-permute-done((bf16[16,128,128]{2,1,0:T(8,128)(2,1)S(1)}, bf16[16,128,128]{2,1,0:T(8,128)(2,1)S(1)}, u32[]{:S(2)}, u32[]{:S(2)}) %collective-permute-start.1) | collective-permute-done | bytes 524320 | tf_op jit(solution)/shard_map/ppermute | solution.py:15
  35.8 3.6 collective-permute-start.2
  39.4 10.2 %collective-permute-done.2 = bf16[16,128,128]{2,1,0:T(8,128)(2,1)S(1)} collective-permute-done((bf16[16,128,128]{2,1,0:T(8,128)(2,1)S(1)}, bf16[16,128,128]{2,1,0:T(8,128)(2,1)S(1)}, u32[]{:S(2)}, u32[]{:S(2)}) %collective-permute-start.2) | collective-permute-done | bytes 524320 | tf_op jit(solution)/shard_map/ppermute | solution.py:15
  50.0 6.1 %collective-permute-start.3 = (bf16[16,128,128]{2,1,0:T(8,128)(2,1)S(1)}, bf16[16,128,128]{2,1,0:T(8,128)(2,1)S(1)}, u32[]{:S(2)}, u32[]{:S(2)}) collective-permute-start(bf16[16,128,128]{2,1,0:T(8,128)(2,1)S(1)} %fusion.69), channel_id=1, source_target_pairs={{0,16},{4,20},{8,24},{12,28},{16,32},{20,36},{24,40},{28,44},{32,4... | collective-permute-start | bytes 1572872 | tf_op jit(solution)/shard_map/ppermute | solution.py:15
  56.1 9.6 %collective-permute-done.3 = bf16[16,128,128]{2,1,0:T(8,128)(2,1)S(1)} collective-permute-done((bf16[16,128,128]{2,1,0:T(8,128)(2,1)S(1)}, bf16[16,128,128]{2,1,0:T(8,128)(2,1)S(1)}, u32[]{:S(2)}, u32[]{:S(2)}) %collective-permute-start.3) | collective-permute-done | bytes 524320 | tf_op jit(solution)/shard_map/ppermute | solution.py:15
  67.0 4.0 %collective-permute-start.4 = (bf16[16,128,128]{2,1,0:T(8,128)(2,1)}, bf16[16,128,128]{2,1,0:T(8,128)(2,1)}, u32[]{:S(2)}, u32[]{:S(2)}) collective-permute-start(bf16[16,128,128]{2,1,0:T(8,128)(2,1)} %fusion.27), channel_id=1, source_target_pairs={{0,32},{4,36},{8,40},{12,44},{16,48},{20,52},{24,56},{28,60},{32,6... | collective-permute-start | bytes 1572872 | tf_op jit(solution)/shard_map/ppermute | solution.py:15
  75.5 3.1 collective-permute-done.4
  78.6 3.1 fusion.68
  81.7 4.1 %collective-permute-start.5 = (bf16[16,128,128]{2,1,0:T(8,128)(2,1)}, bf16[16,128,128]{2,1,0:T(8,128)(2,1)}, u32[]{:S(2)}, u32[]{:S(2)}) collective-permute-start(bf16[16,128,128]{2,1,0:T(8,128)(2,1)} %fusion.68), channel_id=1, source_target_pairs={{0,64},{4,68},{8,72},{12,76},{16,80},{20,84},{24,88},{28,92},{32,9... | collective-permute-start | bytes 1572872 | tf_op jit(solution)/shard_map/ppermute | solution.py:15
  89.8 3.1 convolution_bitcast_fusion.1
  92.8 5.1 %multiply_reduce_fusion = (f32[128,16]{0,1:T(8,128)S(1)}, f32[128,16,128]{0,2,1:T(8,128)S(1)}) fusion(f32[128,16,128]{0,2,1:T(8,128)} %convolution_bitcast_fusion.1, f32[128,16]{0,1:T(8,128)S(1)} %get-tuple-element.12, bf16[16,128,128]{2,1,0:T(8,128)(2,1)} %collective-permute-done.5, f32[16]{0:T(128)} %get-tuple-element.6, ...), kind=kOutput, calls=%fused_computation.22 | convolution fusion | flops 408156160 | bytes 5783872 | tf_op jit(solution)/shard_map/ihd,hde->ihe/dot_general | solution.py:78
  99.0 2.6 copy.65
  105.8 22.1 %all-gather.4.cloned.1.call-done = bf16[320,2048]{1,0:T(8,128)(2,1)} async-done(((bf16[160,2048]{1,0:T(8,128)(2,1)}), bf16[320,2048]{1,0:T(8,128)(2,1)}) %all-gather.4.cloned.1.call-update) | async-done | bytes 1310736 | tf_op jit(solution)/shard_map/all_gather | solution.py:107
  127.9 93.3 %all-gather.6.cloned.1.call-done = bf16[2048,3072]{0,1:T(8,128)(2,1)} async-done(((bf16[2048,192]{0,1:T(8,128)(2,1)}), bf16[2048,3072]{0,1:T(8,128)(2,1)}) %all-gather.6.cloned.1.call-update) | async-done | bytes 12582928 | tf_op jit(solution)/shard_map/all_gather | solution.py:108
  221.2 9.2 %convolution_convert_fusion.1 = bf16[320,3072]{1,0:T(8,128)(2,1)S(1)} fusion(bf16[320,2048]{1,0:T(8,128)(2,1)} %all-gather.4.cloned.1.call-done, bf16[2048,3072]{0,1:T(8,128)(2,1)} %all-gather.6.cloned.1.call-done), kind=kOutput, calls=%fused_computation.3 | convolution fusion | flops 4027514880 | bytes 15859712 | tf_op jit(solution)/shard_map/dot_general | solution.py:110
  232.1 4.4 %all-to-all-start = ((bf16[4,2,1,40,3072]{4,3,1,2,0:T(8,128)(2,1)}), bf16[4,2,1,40,3072]{4,3,1,2,0:T(8,128)(2,1)}, u32[]{:S(2)}, u32[]{:S(2)}) async-start(bf16[4,2,1,40,3072]{4,3,1,2,0:T(8,128)(2,1)} %pad_maximum_fusion), calls=%async_computation | async-start | bytes 3932160 | tf_op jit(solution)/shard_map/all_to_all | solution.py:113
  236.7 2.4 fusion.61
  241.0 19.9 %all-to-all-done = bf16[4,2,1,40,3072]{4,3,1,2,0:T(8,128)(2,1)} async-done(((bf16[4,2,1,40,3072]{4,3,1,2,0:T(8,128)(2,1)}), bf16[4,2,1,40,3072]{4,3,1,2,0:T(8,128)(2,1)}, u32[]{:S(2)}, u32[]{:S(2)}) %all-to-all-start) | async-done | bytes 1966112 | tf_op jit(solution)/shard_map/all_to_all | solution.py:113
  262.9 6.6 %all_to_all.15 = f32[2,40,3072]{2,1,0:T(8,128)} all-to-all(f32[2,40,3072]{2,1,0:T(8,128)S(1)} %convert_reduce_fusion.1), channel_id=1, replica_groups=mesh['yz'=16,'core'=2,'exp'=4] {'core'}, dimensions={0} | all-to-all | bytes 1966080 | tf_op jit(solution)/shard_map/all_to_all | solution.py:116
  269.5 2.9 reshape.213
  272.4 3.5 copy.69
  275.9 3.6 reshape.214
  283.4 43.2 %all-gather.8.cloned.1.call-done = bf16[256,6144]{1,0:T(8,128)(2,1)} async-done(((bf16[8,6144]{1,0:T(8,128)(2,1)}), bf16[256,6144]{1,0:T(8,128)(2,1)}) %all-gather.8.cloned.1.call-update) | async-done | bytes 3145744 | tf_op jit(solution)/shard_map/all_gather | solution.py:132
  326.5 4.8 %fusion.4 = f32[256,288]{0,1:T(8,128)} fusion(bf16[256,6144]{1,0:T(8,128)(2,1)} %all-gather.8.cloned.1.call-done, bf16[1,6144,288]{1,2,0:T(8,128)(2,1)} %param.25), kind=kOutput, calls=%fused_computation.8 | convolution fusion | flops 905969664 | bytes 6979584 | tf_op jit(solution)/shard_map/dot_general | solution.py:133
  331.3 9.4 %fusion = bf16[32,8,6144]{2,1,0:T(8,128)(2,1)} fusion(bf16[1,288,6144]{2,1,0:T(8,128)(2,1)S(1)} %copy-done, bf16[256,6144]{1,0:T(8,128)(2,1)} %all-gather.8.cloned.1.call-done, bf16[1,6144,288]{1,2,0:T(8,128)(2,1)} %param.26, f32[256,288]{0,1:T(8,128)} %fusion.4), kind=kOutput, calls=%fused_computation.1 | convolution fusion | flops 1813954560 | bytes 13664256 | tf_op jit(solution)/shard_map/dot_general | solution.py:136
  340.7 5.4 %all-to-all-start.2 = ((bf16[32,8,6144]{2,1,0:T(8,128)(2,1)}), bf16[32,8,6144]{2,1,0:T(8,128)(2,1)}, u32[]{:S(2)}, u32[]{:S(2)}) async-start(bf16[32,8,6144]{2,1,0:T(8,128)(2,1)} %fusion), calls=%async_computation.2 | async-start | bytes 6291456 | tf_op jit(solution)/shard_map/all_to_all | solution.py:137
  348.1 37.9 %all-to-all-done.2 = bf16[32,8,6144]{2,1,0:T(8,128)(2,1)} async-done(((bf16[32,8,6144]{2,1,0:T(8,128)(2,1)}), bf16[32,8,6144]{2,1,0:T(8,128)(2,1)}, u32[]{:S(2)}, u32[]{:S(2)}) %all-to-all-start.2) | async-done | bytes 3145760 | tf_op jit(solution)/shard_map/all_to_all | solution.py:137
  386.0 2.3 convert_reduce_fusion
  (73 shorter events, 32.6 us)
Async XLA Ops:
  7.2 324.2 %copy-start = (bf16[1,288,6144]{2,1,0:T(8,128)(2,1)S(1)}, bf16[1,288,6144]{2,1,0:T(8,128)(2,1)}, u32[]{:S(2)}) copy-start(bf16[1,288,6144]{2,1,0:T(8,128)(2,1)} %param.27) | copy-start | bytes 10616836
  7.2 120.8 %all-gather.4.cloned.1.call-start = ((), (), s32[]{:S(2)}) async-start(), calls=%async_computation.3 | async-start | bytes 1966080 | tf_op jit(solution)/shard_map/all_gather | solution.py:107
  9.3 56.4 %copy-start.7 = (f32[16]{0:T(128)}, f32[16]{0:T(128)S(1)}, u32[]{:S(2)}) copy-start(f32[16]{0:T(128)S(1)} %get-tuple-element.8) | copy-start | bytes 196
  9.3 69.3 %copy-start.6 = (f32[16]{0:T(128)}, f32[16]{0:T(128)S(1)}, u32[]{:S(2)}) copy-start(f32[16]{0:T(128)S(1)} %get-tuple-element.7) | copy-start | bytes 196
  11.3 54.4 %copy-start.10 = (f32[16]{0:T(128)S(1)}, f32[16]{0:T(128)}, u32[]{:S(2)}) copy-start(f32[16]{0:T(128)} %get-tuple-element.9) | copy-start | bytes 196
  14.0 11.0 %collective-permute-start = (bf16[16,128,128]{2,1,0:T(8,128)(2,1)S(1)}, bf16[16,128,128]{2,1,0:T(8,128)(2,1)S(1)}, u32[]{:S(2)}, u32[]{:S(2)}) collective-permute-start(bf16[16,128,128]{2,1,0:T(8,128)(2,1)S(1)} %convolution_convert_fusion.3), channel_id=1, source_target_pairs={{0,4},{4,8},{8,12},{12,16},{16,20},{20,24},{24,28},{28,32},{32,36}... | collective-permute-start | bytes 1572872 | tf_op jit(solution)/shard_map/ppermute | solution.py:15
  25.0 42.0 %copy-start.1 = (bf16[16,128,128]{2,1,0:T(8,128)(2,1)}, bf16[16,128,128]{2,1,0:T(8,128)(2,1)S(1)}, u32[]{:S(2)}) copy-start(bf16[16,128,128]{2,1,0:T(8,128)(2,1)S(1)} %collective-permute-done) | copy-start | bytes 1572868
  25.0 10.5 %collective-permute-start.1 = (bf16[16,128,128]{2,1,0:T(8,128)(2,1)S(1)}, bf16[16,128,128]{2,1,0:T(8,128)(2,1)S(1)}, u32[]{:S(2)}, u32[]{:S(2)}) collective-permute-start(bf16[16,128,128]{2,1,0:T(8,128)(2,1)S(1)} %collective-permute-done), channel_id=1, source_target_pairs={{0,4},{4,8},{8,12},{12,16},{16,20},{20,24},{24,28},{28,32},{32,36}... | collective-permute-start | bytes 1572872 | tf_op jit(solution)/shard_map/ppermute | solution.py:15
  35.5 31.5 %copy-start.2 = (bf16[16,128,128]{2,1,0:T(8,128)(2,1)}, bf16[16,128,128]{2,1,0:T(8,128)(2,1)S(1)}, u32[]{:S(2)}) copy-start(bf16[16,128,128]{2,1,0:T(8,128)(2,1)S(1)} %collective-permute-done.1) | copy-start | bytes 1572868
  35.5 35.5 %copy-start.12 = (s32[128,2]{0,1:T(2,128)S(1)}, s32[128,2]{0,1:T(2,128)}, u32[]{:S(2)}) copy-start(s32[128,2]{0,1:T(2,128)} %param.23) | copy-start | bytes 3076
  35.8 13.8 %collective-permute-start.2 = (bf16[16,128,128]{2,1,0:T(8,128)(2,1)S(1)}, bf16[16,128,128]{2,1,0:T(8,128)(2,1)S(1)}, u32[]{:S(2)}, u32[]{:S(2)}) collective-permute-start(bf16[16,128,128]{2,1,0:T(8,128)(2,1)S(1)} %fusion.26), channel_id=1, source_target_pairs={{0,8},{4,12},{8,16},{12,20},{16,24},{20,28},{24,32},{28,36},{32,40... | collective-permute-start | bytes 1572872 | tf_op jit(solution)/shard_map/ppermute | solution.py:15
  49.6 21.5 %copy-start.3 = (bf16[16,128,128]{2,1,0:T(8,128)(2,1)}, bf16[16,128,128]{2,1,0:T(8,128)(2,1)S(1)}, u32[]{:S(2)}) copy-start(bf16[16,128,128]{2,1,0:T(8,128)(2,1)S(1)} %collective-permute-done.2) | copy-start | bytes 1572868
  50.0 15.7 %collective-permute-start.3 = (bf16[16,128,128]{2,1,0:T(8,128)(2,1)S(1)}, bf16[16,128,128]{2,1,0:T(8,128)(2,1)S(1)}, u32[]{:S(2)}, u32[]{:S(2)}) collective-permute-start(bf16[16,128,128]{2,1,0:T(8,128)(2,1)S(1)} %fusion.69), channel_id=1, source_target_pairs={{0,16},{4,20},{8,24},{12,28},{16,32},{20,36},{24,40},{28,44},{32,4... | collective-permute-start | bytes 1572872 | tf_op jit(solution)/shard_map/ppermute | solution.py:15
  65.7 5.3 %copy-start.4 = (bf16[16,128,128]{2,1,0:T(8,128)(2,1)}, bf16[16,128,128]{2,1,0:T(8,128)(2,1)S(1)}, u32[]{:S(2)}) copy-start(bf16[16,128,128]{2,1,0:T(8,128)(2,1)S(1)} %collective-permute-done.3) | copy-start | bytes 1572868
  67.0 11.6 %collective-permute-start.4 = (bf16[16,128,128]{2,1,0:T(8,128)(2,1)}, bf16[16,128,128]{2,1,0:T(8,128)(2,1)}, u32[]{:S(2)}, u32[]{:S(2)}) collective-permute-start(bf16[16,128,128]{2,1,0:T(8,128)(2,1)} %fusion.27), channel_id=1, source_target_pairs={{0,32},{4,36},{8,40},{12,44},{16,48},{20,52},{24,56},{28,60},{32,6... | collective-permute-start | bytes 1572872 | tf_op jit(solution)/shard_map/ppermute | solution.py:15
  81.7 11.1 %collective-permute-start.5 = (bf16[16,128,128]{2,1,0:T(8,128)(2,1)}, bf16[16,128,128]{2,1,0:T(8,128)(2,1)}, u32[]{:S(2)}, u32[]{:S(2)}) collective-permute-start(bf16[16,128,128]{2,1,0:T(8,128)(2,1)} %fusion.68), channel_id=1, source_target_pairs={{0,64},{4,68},{8,72},{12,76},{16,80},{20,84},{24,88},{28,92},{32,9... | collective-permute-start | bytes 1572872 | tf_op jit(solution)/shard_map/ppermute | solution.py:15
  97.9 3.7 copy-start.8
  97.9 5.3 %copy-start.9 = (pred[128,4]{0,1:T(4,128)(4,1)S(1)}, pred[128,4]{0,1:T(4,128)(4,1)}, u32[]{:S(2)}) copy-start(pred[128,4]{0,1:T(4,128)(4,1)} %broadcast_compare_fusion) | copy-start | bytes 1540
  105.0 116.2 %all-gather.6.cloned.1.call-start = ((), (), s32[]{:S(2)}) async-start(), calls=%async_computation.4 | async-start | bytes 13369344 | tf_op jit(solution)/shard_map/all_gather | solution.py:108
  230.6 6.0 %copy-start.11 = (s32[32]{0:T(128)S(1)}, s32[32]{0:T(128)}, u32[]{:S(2)}) copy-start(s32[32]{0:T(128)} %eq.56) | copy-start | bytes 388
  232.1 28.8 %all-to-all-start = ((bf16[4,2,1,40,3072]{4,3,1,2,0:T(8,128)(2,1)}), bf16[4,2,1,40,3072]{4,3,1,2,0:T(8,128)(2,1)}, u32[]{:S(2)}, u32[]{:S(2)}) async-start(bf16[4,2,1,40,3072]{4,3,1,2,0:T(8,128)(2,1)} %pad_maximum_fusion), calls=%async_computation | async-start | bytes 3932160 | tf_op jit(solution)/shard_map/all_to_all | solution.py:113
  236.6 90.0 %all-gather.8.cloned.1.call-start = ((), (), s32[]{:S(2)}) async-start(), calls=%async_computation.5 | async-start | bytes 3244032 | tf_op jit(solution)/shard_map/all_gather | solution.py:132
  281.1 0.8 copy-start.5
  340.7 5.5 %copy-start.13 = (s32[128,2]{0,1:T(2,128)S(1)}, s32[128,2]{0,1:T(2,128)}, u32[]{:S(2)}) copy-start(s32[128,2]{0,1:T(2,128)} %param.23) | copy-start | bytes 3076
  340.7 5.5 %copy-start.14 = (f32[128,2]{0,1:T(2,128)S(1)}, f32[128,2]{0,1:T(2,128)}, u32[]{:S(2)}) copy-start(f32[128,2]{0,1:T(2,128)} %param.24) | copy-start | bytes 3076
  340.7 45.3 %all-to-all-start.2 = ((bf16[32,8,6144]{2,1,0:T(8,128)(2,1)}), bf16[32,8,6144]{2,1,0:T(8,128)(2,1)}, u32[]{:S(2)}, u32[]{:S(2)}) async-start(bf16[32,8,6144]{2,1,0:T(8,128)(2,1)} %fusion), calls=%async_computation.2 | async-start | bytes 6291456 | tf_op jit(solution)/shard_map/all_to_all | solution.py:137
Sparse Core Ops, SparseCore 0:
  105.2 22.7 all-gather.3
  130.1 91.0 all-gather.5
  283.5 42.9 all-gather.7
